TPU v7x, 256 devices: a whole 4x4x8 slice. The times are simulated.
256 devices in a mesh: seq: 32 (over x, y, core), tensor: 8 (over z).
Axes of the slice: x: 4, y: 4, z: 8, core: 2. Of those that a mesh axis runs over, the one named last changes fastest.
Arguments:
- tokens: bfloat16 [16384, 4096], P('seq', 'tensor'), may hold values from -6 to 6
- norm_gain: float32 [4096], replicated, may hold values from 0.1 to 1.9
- w_query: bfloat16 [4096, 4096], P('seq', 'tensor'), may hold values from -0.09375 to 0.09375
- w_key: bfloat16 [4096, 4096], P('seq', 'tensor'), may hold values from -0.09375 to 0.09375
- w_value: bfloat16 [4096, 4096], P('seq', 'tensor'), may hold values from -0.09375 to 0.09375
- out_gain: float32 [4096], P('tensor'), may hold values from 0.1 to 1.9
- carried: float32 [32, 128, 128], P('tensor'), may hold values from -384 to 384
Outputs:
- attended: bfloat16 [16384, 4096], P('seq', 'tensor')
- final_state: float32 [32, 128, 128], P('tensor')
All inputs are finite; a program needn't handle non-finite values.
Results may differ from a plain program's by a relative error of at most 0.009.
Values may be sent and summed in bfloat16 or wider, within the bound.
No kernel may reach another device: no remote copies, remote signals or barrier semaphores. Data moves between devices by JAX's collectives and lax.ppermute only.
A program may use at most 64 MiB of HBM per device.

v0:
```python
import jax
import jax.numpy as jnp
from jax import lax
from jax.sharding import PartitionSpec as P

BLOCK = 512


def add_rows(normed, pieces):
    return tuple((jnp.dot(normed, piece, preferred_element_type=jnp.float32) for piece in pieces))


def shards(tokens, norm_gain, w_query, w_key, w_value, out_gain, carried):
    whole = lax.all_gather(tokens, "tensor", axis=1, tiled=True)
    xf = whole.astype(jnp.float32)
    normed = (xf * lax.rsqrt(jnp.mean(xf * xf, axis=1, keepdims=True) + 1e-05) * norm_gain).astype(
        jnp.bfloat16
    )
    rows = normed.shape[0]
    width = w_query.shape[1]
    size = carried.shape[1]
    heads = width // size
    qsum, ksum, vsum = add_rows(
        normed,
        (
            lax.all_gather(w_query, "seq", axis=0, tiled=True),
            lax.all_gather(w_key, "seq", axis=0, tiled=True),
            lax.all_gather(w_value, "seq", axis=0, tiled=True),
        ),
    )
    blocks = rows // BLOCK
    query = qsum.astype(jnp.bfloat16).reshape(blocks, BLOCK, heads, size)
    key = ksum.astype(jnp.bfloat16).reshape(blocks, BLOCK, heads, size)
    value = vsum.astype(jnp.bfloat16).reshape(blocks, BLOCK, heads, size)
    block_state = jnp.einsum("nthd,nthe->nhde", key, value, preferred_element_type=jnp.float32)
    local_total = jnp.sum(block_state, axis=0)
    zero_state = jnp.zeros_like(local_total)
    mine = lax.axis_index("seq")
    piece = lax.all_gather(
        local_total[None].astype(jnp.bfloat16), "seq", axis=0, tiled=True
    ).astype(jnp.float32)
    where = jnp.arange(piece.shape[0], dtype=jnp.int32)
    keep = (where < mine).astype(jnp.float32)
    before = zero_state + jnp.sum(keep[:, None, None, None] * piece, axis=0)
    total = zero_state + jnp.sum(piece, axis=0)
    start_state = carried + before
    running = jnp.cumsum(block_state, axis=0) - block_state
    priors = start_state[None] + running
    inter = jnp.einsum(
        "nthd,nhde->nthe", query.astype(jnp.float32), priors, precision=lax.Precision.HIGHEST
    )
    causal = jnp.tril(jnp.ones((BLOCK, BLOCK), jnp.float32))
    scores = jnp.einsum("nthd,nshd->nhts", query, key, preferred_element_type=jnp.float32)
    weights = (scores * causal).astype(jnp.bfloat16)
    intra = jnp.einsum("nhts,nshe->nthe", weights, value, preferred_element_type=jnp.float32)
    raw = inter + intra
    normal = (
        raw
        * lax.rsqrt(jnp.mean(raw * raw, axis=3, keepdims=True) + 1e-06)
        * out_gain.reshape(heads, size)
    )
    attended = normal.astype(jnp.bfloat16).reshape(rows, width)
    return (attended, carried + total)


def solution(mesh):
    return jax.shard_map(
        shards,
        mesh=mesh,
        in_specs=(
            P("seq", "tensor"),
            P(),
            P("seq", "tensor"),
            P("seq", "tensor"),
            P("seq", "tensor"),
            P("tensor"),
            P("tensor", None, None),
        ),
        out_specs=(P("seq", "tensor"), P("tensor", None, None)),
        check_vma=False,
    )
```

profile of v0, /device:TPU:1, one launch (start us, length us, event | category | flops | bytes accessed | tf_op | source)
XLA Modules:
  0.0 293.1 jit_solution(6839959478735101237)
XLA Ops:
  7.2 0.0 copy-start.4
  7.2 0.0 all-gather.7.cloned.1.call-start
  7.2 0.7 all-gather.7.cloned.1.call-update
  7.9 0.0 all-gather.9.cloned.1.call-start
  8.0 0.7 all-gather.9.cloned.1.call-update
  8.7 0.0 all-gather.11.cloned.1.call-start
  8.7 0.7 all-gather.11.cloned.1.call-update
  9.4 0.0 all-gather.13.cloned.1.call-start
  9.4 0.5 all-gather.13.cloned.1.call-update
  10.0 0.0 all-gather.15.cloned.1.call-start
  10.0 58.4 %all-gather.7.cloned.1.call-done = bf16[512,4096]{1,0:T(8,128)(2,1)} async-done(((bf16[512,512]{1,0:T(8,128)(2,1)}), bf16[512,4096]{1,0:T(8,128)(2,1)}) %all-gather.7.cloned.1.call-update) | async-done | bytes 4194320 | tf_op jit(solution)/shard_map/all_gather | solution.py:14
  68.5 3.1 %fusion = f32[512]{0:T(512)S(1)} fusion(bf16[512,4096]{1,0:T(8,128)(2,1)} %all-gather.7.cloned.1.call-done), kind=kLoop, calls=%fused_computation.4 | loop fusion | flops 6290944 | bytes 4196352 | tf_op jit(solution)/shard_map/reduce_sum | solution.py:16
  71.5 49.6 %all-gather.9.cloned.1.call-done = bf16[4096,512]{1,0:T(8,128)(2,1)} async-done(((bf16[128,512]{1,0:T(8,128)(2,1)}), bf16[4096,512]{1,0:T(8,128)(2,1)}) %all-gather.9.cloned.1.call-update) | async-done | bytes 4194320 | tf_op jit(solution)/shard_map/all_gather | solution.py:27
  121.2 0.0 copy-done.4
  121.2 5.9 %convolution_convert_fusion.2 = bf16[512,512]{0,1:T(8,128)(2,1)S(1)} fusion(bf16[4096,512]{1,0:T(8,128)(2,1)} %all-gather.9.cloned.1.call-done, bf16[512,4096]{1,0:T(8,128)(2,1)} %all-gather.7.cloned.1.call-done, f32[4096]{0:T(1024)S(1)} %copy-done.4, f32[512]{0:T(512)S(1)} %add_rsqrt_fusion.1), kind=kOutput, calls=%fused_computation.14 | convolution fusion | flops 2156134400 | bytes 8931328 | tf_op jit(solution)/shard_map/dot_general | solution.py:10
  127.1 47.2 %all-gather.11.cloned.1.call-done = bf16[4096,512]{1,0:T(8,128)(2,1)} async-done(((bf16[128,512]{1,0:T(8,128)(2,1)}), bf16[4096,512]{1,0:T(8,128)(2,1)}) %all-gather.11.cloned.1.call-update) | async-done | bytes 4194320 | tf_op jit(solution)/shard_map/all_gather | solution.py:28
  174.3 5.9 %convolution_convert_fusion.1 = bf16[512,512]{0,1:T(8,128)(2,1)S(1)} fusion(bf16[4096,512]{1,0:T(8,128)(2,1)} %all-gather.11.cloned.1.call-done, bf16[512,4096]{1,0:T(8,128)(2,1)} %all-gather.7.cloned.1.call-done, f32[4096]{0:T(1024)S(1)} %copy-done.4, f32[512]{0:T(512)S(1)} %add_rsqrt_fusion.1), kind=kOutput, calls=%fused_computation.13 | convolution fusion | flops 2156134400 | bytes 8931328 | tf_op jit(solution)/shard_map/dot_general | solution.py:10
  180.2 1.0 fusion.13
  181.3 0.0 all-gather.15.cloned.1.call-update
  181.3 0.1 fusion.6
  181.4 45.8 %all-gather.13.cloned.1.call-done = bf16[4096,512]{1,0:T(8,128)(2,1)} async-done(((bf16[128,512]{1,0:T(8,128)(2,1)}), bf16[4096,512]{1,0:T(8,128)(2,1)}) %all-gather.13.cloned.1.call-update) | async-done | bytes 4194320 | tf_op jit(solution)/shard_map/all_gather | solution.py:26
  227.2 6.7 %convolution_convert_fusion = bf16[512,512]{0,1:T(8,128)(2,1)} fusion(bf16[4096,512]{1,0:T(8,128)(2,1)} %all-gather.13.cloned.1.call-done, bf16[512,4096]{1,0:T(8,128)(2,1)} %all-gather.7.cloned.1.call-done, f32[4096]{0:T(1024)S(1)} %copy-done.4, f32[512]{0:T(512)S(1)} %add_rsqrt_fusion.1), kind=kOutput, calls=%fused_computation.12 | convolution fusion | flops 2156134400 | bytes 8931328 | tf_op jit(solution)/shard_map/dot_general | solution.py:10
  234.0 2.5 fusion.4
  236.5 0.0 copy-start
  236.5 0.0 copy-start.2
  236.5 0.0 copy-start.3
  236.5 43.7 %all-gather.15.cloned.1.call-done = bf16[128,128,128]{2,1,0:T(8,128)(2,1)} async-done(((bf16[4,128,128]{2,1,0:T(8,128)(2,1)}), bf16[128,128,128]{2,1,0:T(8,128)(2,1)}) %all-gather.15.cloned.1.call-update) | async-done | bytes 4194320 | tf_op jit(solution)/shard_map/all_gather | solution.py:39
  280.2 3.6 %convert_reduce_fusion = (f32[4,128,128]{2,1,0:T(8,128)S(1)}, f32[4,128,128]{2,1,0:T(8,128)S(1)}) fusion(bf16[32,4,128,128]{3,2,1,0:T(8,128)(2,1)} %bitcast.20, f32[32]{0:T(128)S(1)} %compare_convert_fusion), kind=kLoop, calls=%fused_computation | loop fusion | flops 8257536 | bytes 4718720 | tf_op jit(solution)/shard_map/reduce_sum | solution.py:45
  283.9 0.7 multiply_reduce_fusion
  284.6 0.2 multiply_convert_fusion.1
  284.8 1.0 copy.16
  285.8 0.7 add.52
  (8 shorter events, 0.0 us)
Async XLA Ops:
  7.2 114.0 %copy-start.4 = (f32[4096]{0:T(1024)S(1)}, f32[4096]{0:T(1024)}, u32[]{:S(2)}) copy-start(f32[4096]{0:T(1024)} %param.8) | copy-start | bytes 49156
  7.2 61.3 %all-gather.7.cloned.1.call-start = ((), (), s32[]{:S(2)}) async-start(), calls=%async_computation | async-start | bytes 4718592 | tf_op jit(solution)/shard_map/all_gather | solution.py:14
  7.9 113.2 %all-gather.9.cloned.1.call-start = ((), (), s32[]{:S(2)}) async-start(), calls=%async_computation.1 | async-start | bytes 4325376 | tf_op jit(solution)/shard_map/all_gather | solution.py:27
  8.7 165.6 %all-gather.11.cloned.1.call-start = ((), (), s32[]{:S(2)}) async-start(), calls=%async_computation.2 | async-start | bytes 4325376 | tf_op jit(solution)/shard_map/all_gather | solution.py:28
  9.4 217.8 %all-gather.13.cloned.1.call-start = ((), (), s32[]{:S(2)}) async-start(), calls=%async_computation.3 | async-start | bytes 4325376 | tf_op jit(solution)/shard_map/all_gather | solution.py:26
  10.0 270.2 %all-gather.15.cloned.1.call-start = ((), (), s32[]{:S(2)}) async-start(), calls=%async_computation.4 | async-start | bytes 4325376 | tf_op jit(solution)/shard_map/all_gather | solution.py:39
  234.0 49.9 %copy-start.1 = (f32[4,128,128]{2,1,0:T(8,128)S(1)}, f32[4,128,128]{2,1,0:T(8,128)}, u32[]{:S(2)}) copy-start(f32[4,128,128]{2,1,0:T(8,128)} %param.13) | copy-start | bytes 786436
  236.5 47.4 %copy-start = (bf16[512,512]{0,1:T(8,128)(2,1)S(1)}, bf16[512,512]{0,1:T(8,128)(2,1)}, u32[]{:S(2)}) copy-start(bf16[512,512]{0,1:T(8,128)(2,1)} %convolution_convert_fusion) | copy-start | bytes 1572868
  236.5 47.4 %copy-start.2 = (f32[4,128,128]{2,1,0:T(8,128)S(1)}, f32[4,128,128]{2,1,0:T(8,128)}, u32[]{:S(2)}) copy-start(f32[4,128,128]{2,1,0:T(8,128)} %get-tuple-element.9) | copy-start | bytes 786436
  236.5 48.1 %copy-start.3 = (f32[512]{0:T(512)S(1)}, f32[512]{0:T(512)}, u32[]{:S(2)}) copy-start(f32[512]{0:T(512)} %param.12) | copy-start | bytes 6148
Sparse Core Ops, SparseCore 0:
  9.8 58.6 all-gather.6
  71.0 50.0 all-gather.8
  123.7 50.5 all-gather.10
  176.7 50.5 all-gather.12
  229.6 50.5 all-gather.14
where the time goes:
time: 293 us
  waiting for transfers between devices  247 us (84%)
  matrix products  22.9 us (8%)
  between operations  13.9 us (5%)
  other arithmetic  7.74 us (3%)
    all_gather x1, waiting for transfers between devices, shards(): whole = lax.all_gather(tokens, 'tensor', axis=1, tiled=True)  58.4 us
    all_gather x1, waiting for transfers between devices, shards(): lax.all_gather(w_key, 'seq', axis=0, tiled=True)  49.6 us
    all_gather x1, waiting for transfers between devices, shards(): lax.all_gather(w_value, 'seq', axis=0, tiled=True)  47.2 us
    all_gather x1, waiting for transfers between devices, shards(): lax.all_gather(w_query, 'seq', axis=0, tiled=True)  45.8 us
    all_gather x1, waiting for transfers between devices, shards(): lax.all_gather(local_total[None].astype(jnp.bfloat16), 'seq', axis=0, til...  43.7 us
    dot_general x3, matrix products, add_rows(): jnp.dot(normed, piece, preferred_element_type=jnp.float32)  18.6 us
  transfers between devices with their start and end apart: 5, of which 5 were waited for; matrix products, arithmetic and copies ran while one was open for 9% of the time, Pallas kernels for 0%

commit v1 on v0

--- a/solution.py
+++ b/solution.py
@@ -11,7 +11,14 @@
 
 
 def shards(tokens, norm_gain, w_query, w_key, w_value, out_gain, carried):
-    whole = lax.all_gather(tokens, "tensor", axis=1, tiled=True)
+    ring = [tokens]
+    for hop in range(7):
+        ring.append(lax.ppermute(ring[-1], "tensor", [(dev, (dev + 1) % 8) for dev in range(8)]))
+    whole = jnp.roll(
+        jnp.concatenate(ring[::-1], axis=1),
+        (lax.axis_index("tensor") + 1) * ring[0].shape[1],
+        axis=1,
+    )
     xf = whole.astype(jnp.float32)
     normed = (xf * lax.rsqrt(jnp.mean(xf * xf, axis=1, keepdims=True) + 1e-05) * norm_gain).astype(
         jnp.bfloat16

time: 293 us -> 239 us (0.82)
  waiting for transfers between devices: 247 us -> 182 us
  local copies, waits for them, and re-layouts: 1.03 us -> 10.7 us
    ppermute x0 -> x7, waiting for transfers between devices: none -> 85.2 us  [shards(): lax.ppermute(ring[-1], 'tensor', [(dev, (dev + 1) % 8) for dev in range(8)])]
    all_gather x1 -> x0, waiting for transfers between devices: 58.4 us -> none  [shards(): whole = lax.all_gather(tokens, 'tensor', axis=1, tiled=True)]
    all_gather x1, waiting for transfers between devices: 49.6 us -> 0.02 us  [shards(): lax.all_gather(w_key, 'seq', axis=0, tiled=True)]
    all_gather x1, waiting for transfers between devices: 47.2 us -> 4.86 us  [shards(): lax.all_gather(w_value, 'seq', axis=0, tiled=True)]
    unnamed x11 -> x26, local copies, waits for them, and re-layouts: 1.03 us -> 10.6 us
  transfers between devices with their start and end apart: 5 -> 11, of which waited for: 5 -> 10; matrix products, arithmetic and copies ran while one was open for 9% -> 12% of each run, Pallas kernels for 0% -> 0%
where the time goes in v1:
time: 239 us
  waiting for transfers between devices  182 us (76%)
  matrix products  24.1 us (10%)
  between operations  14 us (6%)
  local copies, waits for them, and re-layouts  10.7 us (4%)
  other arithmetic  5.54 us (2%)
  starting transfers between devices  2.71 us (1%)
    ppermute x7, waiting for transfers between devices, shards(): lax.ppermute(ring[-1], 'tensor', [(dev, (dev + 1) % 8) for dev in range(8)])  85.2 us
    all_gather x1, waiting for transfers between devices, shards(): lax.all_gather(w_query, 'seq', axis=0, tiled=True)  46 us
    all_gather x1, waiting for transfers between devices, shards(): lax.all_gather(local_total[None].astype(jnp.bfloat16), 'seq', axis=0, til...  43.8 us
    dot_general x3, matrix products, add_rows(): jnp.dot(normed, piece, preferred_element_type=jnp.float32)  18.8 us
    unnamed x26, local copies, waits for them, and re-layouts  10.6 us
    all_gather x1, waiting for transfers between devices, shards(): lax.all_gather(w_value, 'seq', axis=0, tiled=True)  4.86 us
  transfers between devices with their start and end apart: 11, of which 10 were waited for; matrix products, arithmetic and copies ran while one was open for 12% of the time, Pallas kernels for 0%

profile of v1, /device:TPU:1, one launch (start us, length us, event | category | flops | bytes accessed | tf_op | source)
XLA Modules:
  0.0 239.0 jit_solution(12148023381970950608)
XLA Ops:
  7.2 0.7 all-gather.6.cloned.1.call-update
  8.0 0.7 all-gather.8.cloned.1.call-update
  8.7 0.7 all-gather.10.cloned.1.call-update
  9.4 2.5 %collective-permute-start = (bf16[512,512]{1,0:T(8,128)(2,1)}, bf16[512,512]{1,0:T(8,128)(2,1)S(1)}, u32[]{:S(2)}, u32[]{:S(2)}) collective-permute-start(bf16[512,512]{1,0:T(8,128)(2,1)} %param.7), channel_id=1, source_target_pairs={{0,1},{1,2},{2,3},{3,4},{4,5},{5,6},{6,7},{7,0},{8,9},{9,10},{10,1... | collective-permute-start | bytes 1572872 | tf_op jit(solution)/shard_map/ppermute | solution.py:16
  12.0 15.8 %collective-permute-done = bf16[512,512]{1,0:T(8,128)(2,1)S(1)} collective-permute-done((bf16[512,512]{1,0:T(8,128)(2,1)}, bf16[512,512]{1,0:T(8,128)(2,1)S(1)}, u32[]{:S(2)}, u32[]{:S(2)}) %collective-permute-start) | collective-permute-done | bytes 524320 | tf_op jit(solution)/shard_map/ppermute | solution.py:16
  27.8 13.4 %collective-permute-done.1 = bf16[512,512]{1,0:T(8,128)(2,1)S(1)} collective-permute-done((bf16[512,512]{1,0:T(8,128)(2,1)S(1)}, bf16[512,512]{1,0:T(8,128)(2,1)S(1)}, u32[]{:S(2)}, u32[]{:S(2)}) %collective-permute-start.1) | collective-permute-done | bytes 524320 | tf_op jit(solution)/shard_map/ppermute | solution.py:16
  41.2 12.6 %collective-permute-done.2 = bf16[512,512]{1,0:T(8,128)(2,1)S(1)} collective-permute-done((bf16[512,512]{1,0:T(8,128)(2,1)S(1)}, bf16[512,512]{1,0:T(8,128)(2,1)S(1)}, u32[]{:S(2)}, u32[]{:S(2)}) %collective-permute-start.2) | collective-permute-done | bytes 524320 | tf_op jit(solution)/shard_map/ppermute | solution.py:16
  53.8 11.7 %collective-permute-done.3 = bf16[512,512]{1,0:T(8,128)(2,1)S(1)} collective-permute-done((bf16[512,512]{1,0:T(8,128)(2,1)S(1)}, bf16[512,512]{1,0:T(8,128)(2,1)S(1)}, u32[]{:S(2)}, u32[]{:S(2)}) %collective-permute-start.3) | collective-permute-done | bytes 524320 | tf_op jit(solution)/shard_map/ppermute | solution.py:16
  65.4 10.7 %collective-permute-done.4 = bf16[512,512]{1,0:T(8,128)(2,1)S(1)} collective-permute-done((bf16[512,512]{1,0:T(8,128)(2,1)S(1)}, bf16[512,512]{1,0:T(8,128)(2,1)S(1)}, u32[]{:S(2)}, u32[]{:S(2)}) %collective-permute-start.4) | collective-permute-done | bytes 524320 | tf_op jit(solution)/shard_map/ppermute | solution.py:16
  76.2 10.5 %collective-permute-done.5 = bf16[512,512]{1,0:T(8,128)(2,1)} collective-permute-done((bf16[512,512]{1,0:T(8,128)(2,1)S(1)}, bf16[512,512]{1,0:T(8,128)(2,1)}, u32[]{:S(2)}, u32[]{:S(2)}) %collective-permute-start.5) | collective-permute-done | bytes 524320 | tf_op jit(solution)/shard_map/ppermute | solution.py:16
  86.7 10.6 %collective-permute-done.6 = bf16[512,512]{1,0:T(8,128)(2,1)} collective-permute-done((bf16[512,512]{1,0:T(8,128)(2,1)}, bf16[512,512]{1,0:T(8,128)(2,1)}, u32[]{:S(2)}, u32[]{:S(2)}) %collective-permute-start.6) | collective-permute-done | bytes 524320 | tf_op jit(solution)/shard_map/ppermute | solution.py:16
  97.2 1.1 constant_dynamic-update-slice_fusion.15
  98.4 1.1 constant_dynamic-update-slice_fusion.14
  99.9 1.1 constant_dynamic-update-slice_fusion.8
  101.0 1.1 constant_dynamic-update-slice_fusion.7
  102.1 1.2 constant_dynamic-update-slice_fusion.6
  103.8 3.2 %copy-done = bf16[512,8192]{1,0:T(8,128)(2,1)} copy-done((bf16[512,8192]{1,0:T(8,128)(2,1)}, bf16[512,8192]{1,0:T(8,128)(2,1)S(1)}, u32[]{:S(2)}) %copy-start) | copy-done | bytes 8388632
  107.0 0.9 fusion
  108.0 6.2 %convolution_convert_fusion.2 = bf16[512,512]{0,1:T(8,128)(2,1)S(1)} fusion(bf16[4096,512]{1,0:T(8,128)(2,1)} %all-gather.6.cloned.1.call-done, f32[4096]{0:T(1024)S(1)} %copy-done.4, f32[512]{0:T(512)S(1)} %add_rsqrt_fusion.1, bf16[512,8192]{1,0:T(8,128)(2,1)} %copy-done, s32[]{:T(128)S(6)} %select_n.22), kind=kOutput, calls=%fused_computation.14 | convolution fusion | flops 2156134400 | bytes 8931332 | tf_op jit(solution)/shard_map/dot_general | solution.py:10
  114.1 4.9 %all-gather.8.cloned.1.call-done = bf16[4096,512]{1,0:T(8,128)(2,1)} async-done(((bf16[128,512]{1,0:T(8,128)(2,1)}), bf16[4096,512]{1,0:T(8,128)(2,1)}) %all-gather.8.cloned.1.call-update) | async-done | bytes 4194320 | tf_op jit(solution)/shard_map/all_gather | solution.py:35
  119.0 5.9 %convolution_convert_fusion.1 = bf16[512,512]{0,1:T(8,128)(2,1)S(1)} fusion(bf16[4096,512]{1,0:T(8,128)(2,1)} %all-gather.8.cloned.1.call-done, f32[4096]{0:T(1024)S(1)} %copy-done.4, f32[512]{0:T(512)S(1)} %add_rsqrt_fusion.1, bf16[512,8192]{1,0:T(8,128)(2,1)} %copy-done, s32[]{:T(128)S(6)} %select_n.22), kind=kOutput, calls=%fused_computation.13 | convolution fusion | flops 2156134400 | bytes 8931332 | tf_op jit(solution)/shard_map/dot_general | solution.py:10
  124.9 1.0 fusion.13
  126.0 0.1 fusion.6
  126.2 46.0 %all-gather.10.cloned.1.call-done = bf16[4096,512]{1,0:T(8,128)(2,1)} async-done(((bf16[128,512]{1,0:T(8,128)(2,1)}), bf16[4096,512]{1,0:T(8,128)(2,1)}) %all-gather.10.cloned.1.call-update) | async-done | bytes 4194320 | tf_op jit(solution)/shard_map/all_gather | solution.py:33
  172.1 6.7 %convolution_convert_fusion = bf16[512,512]{0,1:T(8,128)(2,1)} fusion(bf16[4096,512]{1,0:T(8,128)(2,1)} %all-gather.10.cloned.1.call-done, f32[4096]{0:T(1024)S(1)} %copy-done.4, f32[512]{0:T(512)S(1)} %add_rsqrt_fusion.1, bf16[512,8192]{1,0:T(8,128)(2,1)} %copy-done, s32[]{:T(128)S(6)} %select_n.22), kind=kOutput, calls=%fused_computation.12 | convolution fusion | flops 2156134400 | bytes 8931332 | tf_op jit(solution)/shard_map/dot_general | solution.py:10
  178.9 2.4 %fusion.4 = f32[4,128,512]{2,1,0:T(8,128)S(1)} fusion(bf16[512,4,128]{0,2,1:T(8,128)(2,1)S(1)} %bitcast.24, bf16[512,4,128]{0,2,1:T(8,128)(2,1)} %bitcast.25, bf16[512,4,128]{0,2,1:T(8,128)(2,1)S(1)} %bitcast.22, f32[512,512]{1,0:T(8,128)S(1)} %fusion.6), kind=kOutput, calls=%fused_computation.9 | convolution fusion | flops 538968064 | bytes 3670016 | tf_op jit(solution)/shard_map/nhts,nshe->nthe/dot_general | solution.py:62
  181.3 43.8 %all-gather.12.cloned.1.call-done = bf16[128,128,128]{2,1,0:T(8,128)(2,1)} async-done(((bf16[4,128,128]{2,1,0:T(8,128)(2,1)}), bf16[128,128,128]{2,1,0:T(8,128)(2,1)}) %all-gather.12.cloned.1.call-update) | async-done | bytes 4194320 | tf_op jit(solution)/shard_map/all_gather | solution.py:46
  225.1 3.6 %convert_reduce_fusion = (f32[4,128,128]{2,1,0:T(8,128)S(1)}, f32[4,128,128]{2,1,0:T(8,128)S(1)}) fusion(bf16[32,4,128,128]{3,2,1,0:T(8,128)(2,1)} %bitcast.20, f32[32]{0:T(128)S(1)} %compare_convert_fusion), kind=kLoop, calls=%fused_computation | loop fusion | flops 8257536 | bytes 4718720 | tf_op jit(solution)/shard_map/reduce_sum | solution.py:52
  228.8 1.8 multiply_reduce_fusion
  230.6 0.2 multiply_convert_fusion.1
  230.8 1.0 copy.16
  231.8 0.7 add.68
  (35 shorter events, 1.0 us)
Async XLA Ops:
  7.2 96.6 %copy-start.1 = (bf16[512,512]{1,0:T(8,128)(2,1)S(1)}, bf16[512,512]{1,0:T(8,128)(2,1)}, u32[]{:S(2)}) copy-start(bf16[512,512]{1,0:T(8,128)(2,1)} %param.7) | copy-start | bytes 1572868
  7.2 100.8 %all-gather.6.cloned.1.call-start = ((), (), s32[]{:S(2)}) async-start(), calls=%async_computation | async-start | bytes 4325376 | tf_op jit(solution)/shard_map/all_gather | solution.py:34
  7.9 111.1 %all-gather.8.cloned.1.call-start = ((), (), s32[]{:S(2)}) async-start(), calls=%async_computation.1 | async-start | bytes 4325376 | tf_op jit(solution)/shard_map/all_gather | solution.py:35
  8.7 163.5 %all-gather.10.cloned.1.call-start = ((), (), s32[]{:S(2)}) async-start(), calls=%async_computation.2 | async-start | bytes 4325376 | tf_op jit(solution)/shard_map/all_gather | solution.py:33
  9.4 215.7 %all-gather.12.cloned.1.call-start = ((), (), s32[]{:S(2)}) async-start(), calls=%async_computation.3 | async-start | bytes 4325376 | tf_op jit(solution)/shard_map/all_gather | solution.py:46
  9.4 18.3 %collective-permute-start = (bf16[512,512]{1,0:T(8,128)(2,1)}, bf16[512,512]{1,0:T(8,128)(2,1)S(1)}, u32[]{:S(2)}, u32[]{:S(2)}) collective-permute-start(bf16[512,512]{1,0:T(8,128)(2,1)} %param.7), channel_id=1, source_target_pairs={{0,1},{1,2},{2,3},{3,4},{4,5},{5,6},{6,7},{7,0},{8,9},{9,10},{10,1... | collective-permute-start | bytes 1572872 | tf_op jit(solution)/shard_map/ppermute | solution.py:16
  27.8 13.4 %collective-permute-start.1 = (bf16[512,512]{1,0:T(8,128)(2,1)S(1)}, bf16[512,512]{1,0:T(8,128)(2,1)S(1)}, u32[]{:S(2)}, u32[]{:S(2)}) collective-permute-start(bf16[512,512]{1,0:T(8,128)(2,1)S(1)} %collective-permute-done), channel_id=1, source_target_pairs={{0,1},{1,2},{2,3},{3,4},{4,5},{5,6},{6,7},{7,0},{8,9},{9,10},{10,1... | collective-permute-start | bytes 1572872 | tf_op jit(solution)/shard_map/ppermute | solution.py:16
  41.2 12.6 %collective-permute-start.2 = (bf16[512,512]{1,0:T(8,128)(2,1)S(1)}, bf16[512,512]{1,0:T(8,128)(2,1)S(1)}, u32[]{:S(2)}, u32[]{:S(2)}) collective-permute-start(bf16[512,512]{1,0:T(8,128)(2,1)S(1)} %collective-permute-done.1), channel_id=1, source_target_pairs={{0,1},{1,2},{2,3},{3,4},{4,5},{5,6},{6,7},{7,0},{8,9},{9,10},{10,1... | collective-permute-start | bytes 1572872 | tf_op jit(solution)/shard_map/ppermute | solution.py:16
  53.8 11.7 %collective-permute-start.3 = (bf16[512,512]{1,0:T(8,128)(2,1)S(1)}, bf16[512,512]{1,0:T(8,128)(2,1)S(1)}, u32[]{:S(2)}, u32[]{:S(2)}) collective-permute-start(bf16[512,512]{1,0:T(8,128)(2,1)S(1)} %collective-permute-done.2), channel_id=1, source_target_pairs={{0,1},{1,2},{2,3},{3,4},{4,5},{5,6},{6,7},{7,0},{8,9},{9,10},{10,1... | collective-permute-start | bytes 1572872 | tf_op jit(solution)/shard_map/ppermute | solution.py:16
  65.4 10.7 %collective-permute-start.4 = (bf16[512,512]{1,0:T(8,128)(2,1)S(1)}, bf16[512,512]{1,0:T(8,128)(2,1)S(1)}, u32[]{:S(2)}, u32[]{:S(2)}) collective-permute-start(bf16[512,512]{1,0:T(8,128)(2,1)S(1)} %collective-permute-done.3), channel_id=1, source_target_pairs={{0,1},{1,2},{2,3},{3,4},{4,5},{5,6},{6,7},{7,0},{8,9},{9,10},{10,1... | collective-permute-start | bytes 1572872 | tf_op jit(solution)/shard_map/ppermute | solution.py:16
  76.2 10.5 %collective-permute-start.5 = (bf16[512,512]{1,0:T(8,128)(2,1)S(1)}, bf16[512,512]{1,0:T(8,128)(2,1)}, u32[]{:S(2)}, u32[]{:S(2)}) collective-permute-start(bf16[512,512]{1,0:T(8,128)(2,1)S(1)} %collective-permute-done.4), channel_id=1, source_target_pairs={{0,1},{1,2},{2,3},{3,4},{4,5},{5,6},{6,7},{7,0},{8,9},{9,10},{10,1... | collective-permute-start | bytes 1572872 | tf_op jit(solution)/shard_map/ppermute | solution.py:16
  86.7 10.6 %collective-permute-start.6 = (bf16[512,512]{1,0:T(8,128)(2,1)}, bf16[512,512]{1,0:T(8,128)(2,1)}, u32[]{:S(2)}, u32[]{:S(2)}) collective-permute-start(bf16[512,512]{1,0:T(8,128)(2,1)} %collective-permute-done.5), channel_id=1, source_target_pairs={{0,1},{1,2},{2,3},{3,4},{4,5},{5,6},{6,7},{7,0},{8,9},{9,10},{10,1... | collective-permute-start | bytes 1572872 | tf_op jit(solution)/shard_map/ppermute | solution.py:16
  99.6 8.3 %copy-start.4 = (f32[4096]{0:T(1024)S(1)}, f32[4096]{0:T(1024)}, u32[]{:S(2)}) copy-start(f32[4096]{0:T(1024)} %param.8) | copy-start | bytes 49156
  103.8 3.2 %copy-start = (bf16[512,8192]{1,0:T(8,128)(2,1)}, bf16[512,8192]{1,0:T(8,128)(2,1)S(1)}, u32[]{:S(2)}) copy-start(bf16[512,8192]{1,0:T(8,128)(2,1)S(1)} %constant_dynamic-update-slice_fusion) | copy-start | bytes 25165828
  126.2 102.6 %copy-start.2 = (f32[4,128,128]{2,1,0:T(8,128)S(1)}, f32[4,128,128]{2,1,0:T(8,128)}, u32[]{:S(2)}) copy-start(f32[4,128,128]{2,1,0:T(8,128)} %param.13) | copy-start | bytes 786436
  178.9 51.7 %copy-start.3 = (f32[512]{0:T(512)S(1)}, f32[512]{0:T(512)}, u32[]{:S(2)}) copy-start(f32[512]{0:T(512)} %param.12) | copy-start | bytes 6148
Sparse Core Ops, SparseCore 0:
  10.6 55.2 all-gather.5
  68.5 50.5 all-gather.7
  121.6 50.5 all-gather.9
  174.5 50.5 all-gather.11
